TPU v7x, 32 devices: a whole 2x2x4 slice. The times are simulated.
32 devices in a mesh: tm: 2 (over y), height: 16 (over z, x, core).
Axes of the slice: x: 2, y: 2, z: 4, core: 2. Of those that a mesh axis runs over, the one named last changes fastest.
Arguments:
- activations: bfloat16 [4, 64, 256, 128], P('tm', 'height'), may hold values from -60 to 60
- norm_gain: float32 [128], replicated, may hold values from 0.1 to 1.9
- norm_bias: float32 [128], replicated, may hold values from -3 to 3
- conv_weight: bfloat16 [3456, 256], replicated, may hold values from -0.109375 to 0.109375
- cotangent: bfloat16 [2, 64, 256, 256], P('tm', 'height'), may hold values from -6 to 6
Outputs:
- pooled: bfloat16 [2, 64, 256, 256], P('tm', None, 'height')
- weight_grad: bfloat16 [256, 3456], P('height')
All inputs are finite; a program needn't handle non-finite values.
Results may differ from a plain program's by a relative error of at most 0.0056.
Values may be sent and summed in bfloat16 or wider, within the bound.
A program may use at most 128 MiB of HBM per device.

v0:
```python
import math
import jax
import jax.numpy as jnp
from jax import lax
from jax.sharding import PartitionSpec as P

GROUPS = 32
KT = 3


def shifted(value, axis, steps):
    count = lax.axis_size(axis)
    first, last = (max(0, -steps), min(count, count - steps))
    return lax.ppermute(value, axis, [(source, source + steps) for source in range(first, last)])


def extended(cells, sides, width):
    for axis, dim in sides:
        count = lax.axis_size(axis)
        ends = count - 1
        head = lax.slice_in_dim(cells, 0, width, axis=dim)
        tail = lax.slice_in_dim(cells, cells.shape[dim] - width, cells.shape[dim], axis=dim)
        cells = jnp.concatenate(
            [
                lax.ppermute(tail, axis, [(i, (i + 1) % count) for i in range(ends)]),
                cells,
                lax.ppermute(head, axis, [((i + 1) % count, i) for i in range(ends)]),
            ],
            axis=dim,
        )
    return cells


def pool_pairs(values):
    paired = values.reshape((values.shape[0] // 2, 2) + values.shape[1:])
    return ((paired[:, 0].astype(jnp.float32) + paired[:, 1].astype(jnp.float32)) * 0.5).astype(
        jnp.bfloat16
    )


def local(activations, norm_gain, norm_bias, conv_weight, cotangent):
    frames, rows, width, channels = activations.shape
    n_out = conv_weight.shape[1]
    per_group = channels // GROUPS
    n_time = lax.axis_size("tm")
    n_rows = lax.axis_size("height")
    entries = frames * rows * width * per_group * n_time * n_rows
    grouped = activations.reshape(frames * rows * width, GROUPS, per_group)
    local_sums = jnp.sum(grouped, axis=(0, 2), dtype=jnp.float32)
    group_mean = lax.psum(local_sums, ("tm", "height")) / entries
    centered = grouped.astype(jnp.float32) - group_mean[None, :, None]
    group_var = lax.psum(jnp.sum(centered * centered, axis=(0, 2)), ("tm", "height")) / entries
    mean_chan = jnp.repeat(group_mean, per_group)
    inv_chan = jnp.repeat(lax.rsqrt(group_var + 1e-06), per_group)
    normed = jax.nn.silu(
        (activations.astype(jnp.float32) - mean_chan) * inv_chan * norm_gain + norm_bias
    ).astype(jnp.bfloat16)
    earlier = shifted(normed, "tm", 1)
    first_frame = jnp.broadcast_to(normed[:1], earlier.shape)
    earlier = jnp.where(lax.axis_index("tm") == 0, first_frame, earlier)
    stacked = jnp.concatenate([earlier, normed], axis=0)
    padded = extended(stacked, (("height", 1),), 1)
    padded = jnp.pad(padded, ((0, 0), (0, 0), (1, 1), (0, 0)))
    patches = jnp.concatenate([padded[:, :, tap_c : tap_c + width] for tap_c in range(KT)], axis=3)
    band = KT * channels
    output = jnp.zeros((frames, rows, n_out, width), jnp.float32)
    for tap_t in range(KT):
        for tap_r in range(KT):
            start_row = (tap_t * KT + tap_r) * band
            output = output + jnp.einsum(
                "frwk,kc->frcw",
                patches[tap_t : tap_t + frames, tap_r : tap_r + rows],
                conv_weight[start_row : start_row + band],
                preferred_element_type=jnp.float32,
            )
    conv_out = output.astype(jnp.bfloat16)
    moved = lax.all_to_all(conv_out, "height", split_axis=2, concat_axis=1, tiled=True)
    pooled = pool_pairs(moved)
    upsampled = jnp.repeat(cotangent * jnp.asarray(0.5, jnp.bfloat16), 2, axis=0)
    own_rows = n_out // n_rows
    blocks = []
    for tap_t in range(KT):
        for tap_r in range(KT):
            blocks.append(
                jnp.einsum(
                    "frwk,frwc->ck",
                    patches[tap_t : tap_t + frames, tap_r : tap_r + rows],
                    upsampled,
                    preferred_element_type=jnp.float32,
                )
            )
    summed = lax.psum(jnp.concatenate(blocks, axis=1), ("tm", "height"))
    own_grad = lax.dynamic_slice_in_dim(summed, lax.axis_index("height") * own_rows, own_rows, 0)
    factor = 1.0 / math.sqrt(frames * n_time * rows * n_rows * width)
    weight_grad = (own_grad * factor).astype(jnp.bfloat16)
    return (pooled, weight_grad)


def solution(mesh):
    in_specs = (P("tm", "height", None, None), P(), P(), P(), P("tm", "height", None, None))
    out_specs = (P("tm", None, "height", None), P("height", None))
    return jax.shard_map(local, mesh=mesh, in_specs=in_specs, out_specs=out_specs, check_vma=False)
```

profile of v0, /device:TPU:0, one launch (start us, length us, event | category | flops | bytes accessed | tf_op | source)
XLA Modules:
  0.0 317.6 jit_solution(3643180153994988676)
XLA Ops:
  7.2 1.4 convert_reduce_fusion
  8.8 42.0 %psum.21 = f32[32]{0:T(128)S(1)} all-reduce(f32[32]{0:T(128)S(1)} %reduce_sum.25), channel_id=1, replica_groups=mesh['tm'=2,'height'=16] {'tm','height'}, use_global_device_ids=true, to_apply=%region_2.0 | all-reduce | flops 32 | bytes 256 | tf_op jit(solution)/shard_map/psum | solution.py:50
  51.0 1.3 fusion.79
  52.6 40.2 %psum.22 = f32[32]{0:T(128)S(1)} all-reduce(f32[32]{0:T(128)S(1)} %reduce_sum.37), channel_id=1, replica_groups=mesh['tm'=2,'height'=16] {'tm','height'}, use_global_device_ids=true, to_apply=%region_5.6 | all-reduce | flops 32 | bytes 256 | tf_op jit(solution)/shard_map/psum | solution.py:52
  92.9 1.4 fusion.87
  94.4 4.2 %collective-permute-start = (bf16[2,4,256,128]{3,2,1,0:T(8,128)(2,1)S(1)}, bf16[2,4,256,128]{3,2,1,0:T(8,128)(2,1)S(1)}, u32[]{:S(2)}, u32[]{:S(2)}) collective-permute-start(bf16[2,4,256,128]{3,2,1,0:T(8,128)(2,1)S(1)} %fusion.87), channel_id=1, source_target_pairs={{0,16},{1,17},{2,18},{3,19},{4,20},{5,21},{6,22},{7,23},{8,24},{9,... | collective-permute-start | bytes 1572872 | tf_op jit(solution)/shard_map/ppermute | solution.py:14
  98.6 10.2 %collective-permute-done = bf16[2,4,256,128]{3,2,1,0:T(8,128)(2,1)S(1)} collective-permute-done((bf16[2,4,256,128]{3,2,1,0:T(8,128)(2,1)S(1)}, bf16[2,4,256,128]{3,2,1,0:T(8,128)(2,1)S(1)}, u32[]{:S(2)}, u32[]{:S(2)}) %collective-permute-start) | collective-permute-done | bytes 524320 | tf_op jit(solution)/shard_map/ppermute | solution.py:14
  109.0 1.3 collective-permute-start.2
  110.3 3.0 collective-permute-start.1
  114.9 1.1 fusion.124
  116.0 2.1 pad_maximum_fusion
  118.8 2.2 fusion.101
  121.0 2.0 fusion.103
  123.0 2.0 fusion.105
  125.0 2.0 fusion.107
  127.0 2.1 fusion.109
  129.1 2.1 fusion.113
  131.1 2.1 fusion.111
  133.2 1.5 fusion.28
  134.7 1.5 fusion.34
  136.2 1.5 fusion.40
  137.8 1.5 fusion.46
  139.3 1.5 fusion.52
  140.7 1.5 fusion.58
  142.3 1.6 fusion.64
  143.8 1.5 fusion.70
  145.3 1.5 fusion.76
  146.9 6.7 %fusion.22 = bf16[2,4,256,256]{2,3,1,0:T(8,128)(2,1)S(1)} fusion(bf16[4,6,256,384]{3,2,1,0:T(8,128)(2,1)} %copy-done, f32[2,4,256,256]{3,2,1,0:T(8,128)S(1)} %fusion.99, f32[2,4,256,256]{3,2,1,0:T(8,128)} %fusion.101, f32[2,4,256,256]{3,2,1,0:T(8,128)} %fusion.103, f32[2,4,256,256]{3,2,1,0:T(8,128)} %fusion.105, f32[2,4,256,256]{3,2,1,0:T(8,128)} %fusion.107, ...), kind=kOutput, calls=%fused_computation.28 | convolution fusion | flops 407371776 | bytes 22740992 | tf_op jit(solution)/shard_map/frwk,kc->frcw/dot_general | solution.py:70
  153.6 1.8 copy.14
  155.4 8.7 %all-to-all-start = ((bf16[2,4,256,256]{3,1,0,2:T(4,128)(2,1)}), bf16[2,4,256,256]{3,1,0,2:T(4,128)(2,1)S(1)}, u32[]{:S(2)}, u32[]{:S(2)}) async-start(bf16[2,4,256,256]{3,1,0,2:T(4,128)(2,1)} %copy.14), calls=%async_computation | async-start | bytes 2097152 | tf_op jit(solution)/shard_map/all_to_all | solution.py:77
  164.2 143.7 %all-reduce.3.cloned.1.call-done = f32[256,3456]{1,0:T(8,128)} async-done(((f32[256,3456]{1,0:T(8,128)}), f32[256,3456]{1,0:T(8,128)}) %all-reduce.3.cloned.1.call-update) | async-done | bytes 3538960 | tf_op jit(solution)/shard_map/psum | solution.py:92
  307.8 1.6 multiply_convert_fusion.1
  (31 shorter events, 4.5 us)
Async XLA Ops:
  7.2 106.2 %copy-start.2 = (bf16[1,4,256,256]{3,2,1,0:T(8,128)(2,1)S(1)}, bf16[1,4,256,256]{3,2,1,0:T(8,128)(2,1)}, u32[]{:S(2)}) copy-start(bf16[1,4,256,256]{3,2,1,0:T(8,128)(2,1)} %param.9) | copy-start | bytes 1572868
  7.2 300.7 %all-reduce.3.cloned.1.call-start = ((), (), s32[]{:S(2)}) async-start(), calls=%async_computation.1 | async-start | bytes 7077888 | tf_op jit(solution)/shard_map/psum | solution.py:92
  94.4 14.5 %collective-permute-start = (bf16[2,4,256,128]{3,2,1,0:T(8,128)(2,1)S(1)}, bf16[2,4,256,128]{3,2,1,0:T(8,128)(2,1)S(1)}, u32[]{:S(2)}, u32[]{:S(2)}) collective-permute-start(bf16[2,4,256,128]{3,2,1,0:T(8,128)(2,1)S(1)} %fusion.87), channel_id=1, source_target_pairs={{0,16},{1,17},{2,18},{3,19},{4,20},{5,21},{6,22},{7,23},{8,24},{9,... | collective-permute-start | bytes 1572872 | tf_op jit(solution)/shard_map/ppermute | solution.py:14
  109.0 4.6 %collective-permute-start.2 = (bf16[4,1,256,128]{3,2,1,0:T(8,128)(2,1)S(1)}, bf16[4,1,256,128]{3,2,1,0:T(8,128)(2,1)S(1)}, u32[]{:S(2)}, u32[]{:S(2)}) collective-permute-start(bf16[4,1,256,128]{3,2,1,0:T(8,128)(2,1)S(1)} %get-tuple-element.5), channel_id=1, source_target_pairs={{1,0},{2,1},{3,2},{4,3},{5,4},{6,5},{7,6},{8,7},{9,8},{10,9},{11,1... | collective-permute-start | bytes 786440 | tf_op jit(solution)/shard_map/ppermute | solution.py:27
  110.3 4.2 %collective-permute-start.1 = (bf16[4,1,256,128]{3,2,1,0:T(8,128)(2,1)S(1)}, bf16[4,1,256,128]{3,2,1,0:T(8,128)(2,1)S(1)}, u32[]{:S(2)}, u32[]{:S(2)}) collective-permute-start(bf16[4,1,256,128]{3,2,1,0:T(8,128)(2,1)S(1)} %get-tuple-element.4), channel_id=1, source_target_pairs={{0,1},{1,2},{2,3},{3,4},{4,5},{5,6},{6,7},{7,8},{8,9},{9,10},{10,1... | collective-permute-start | bytes 786440 | tf_op jit(solution)/shard_map/ppermute | solution.py:25
  116.0 2.1 copy-start.1
  118.1 27.2 %copy-start = (bf16[4,6,256,384]{3,2,1,0:T(8,128)(2,1)}, bf16[4,6,256,384]{3,2,1,0:T(8,128)(2,1)S(1)}, u32[]{:S(2)}) copy-start(bf16[4,6,256,384]{3,2,1,0:T(8,128)(2,1)S(1)} %pad_maximum_fusion) | copy-start | bytes 14155780
  155.4 154.0 %all-to-all-start = ((bf16[2,4,256,256]{3,1,0,2:T(4,128)(2,1)}), bf16[2,4,256,256]{3,1,0,2:T(4,128)(2,1)S(1)}, u32[]{:S(2)}, u32[]{:S(2)}) async-start(bf16[2,4,256,256]{3,1,0,2:T(4,128)(2,1)} %copy.14), calls=%async_computation | async-start | bytes 2097152 | tf_op jit(solution)/shard_map/all_to_all | solution.py:77
Sparse Core Ops, SparseCore 0:
  147.0 160.7 all-reduce.2
where the time goes:
time: 318 us
  waiting for transfers between devices  155 us (49%)
  blocking collectives  82.2 us (26%)
  matrix products  35.4 us (11%)
  starting transfers between devices  17.3 us (5%)
  between operations  14.2 us (4%)
  other arithmetic  9.63 us (3%)
  local copies, waits for them, and re-layouts  4.02 us (1%)
    psum x1, waiting for transfers between devices, local(): summed = lax.psum(jnp.concatenate(blocks, axis=1), ('tm', 'height'))  144 us
    psum x1, blocking collectives, local(): group_mean = lax.psum(local_sums, ('tm', 'height')) / entries  42 us
    psum x1, blocking collectives, local(): lax.psum(jnp.sum(centered * centered, axis=(0, 2)), ('tm', 'height'))  40.2 us
    dot_general x9, matrix products, local(): jnp.einsum('frwk,kc->frcw', patches[tap_t:tap_t + frames, tap_r:tap_r + r...  21.8 us
    dot_general x9, matrix products, local(): jnp.einsum('frwk,frwc->ck', patches[tap_t:tap_t + frames, tap_r:tap_r + r...  13.6 us
    ppermute x1, waiting for transfers between devices, shifted(): lax.ppermute(value, axis, [(source, source + steps) for source in range(f...  10.2 us
    all_to_all x1, starting transfers between devices, local(): lax.all_to_all(conv_out, 'height', split_axis=2, concat_axis=1, tiled=True)  8.75 us
  transfers between devices with their start and end apart: 5, of which 3 were waited for; matrix products, arithmetic and copies ran while one was open for 3% of the time, Pallas kernels for 0%

commit v1 on v0

--- a/solution.py
+++ b/solution.py
@@ -6,6 +6,29 @@
 
 GROUPS = 32
 KT = 3
+
+
+def split_up(value, dim, size):
+    before, after = (value.shape[:dim], value.shape[dim + 1 :])
+    return jnp.moveaxis(value.reshape(*before, size, -1, *after), dim, 0)
+
+
+def in_order(parts, dim):
+    parts = jnp.moveaxis(parts, 0, dim)
+    lengths = parts.shape
+    return parts.reshape(*lengths[:dim], lengths[dim] * lengths[dim + 1], *lengths[dim + 2 :])
+
+
+def rotated_exchange(shard, axis, split_dim, concat_dim):
+    size, mine = (lax.axis_size(axis), lax.axis_index(axis))
+    blocks = split_up(shard, split_dim, size)
+    out = blocks
+    for step in range(1, size):
+        target, source = ((mine + step) % size, (mine - step) % size)
+        sent = lax.dynamic_index_in_dim(blocks, target, 0)
+        other = lax.ppermute(sent, axis, [(i, (i + step) % size) for i in range(size)])
+        out = lax.dynamic_update_slice_in_dim(out, other, source, axis=0)
+    return in_order(out, concat_dim)
 
 
 def shifted(value, axis, steps):
@@ -74,7 +97,7 @@
                 preferred_element_type=jnp.float32,
             )
     conv_out = output.astype(jnp.bfloat16)
-    moved = lax.all_to_all(conv_out, "height", split_axis=2, concat_axis=1, tiled=True)
+    moved = rotated_exchange(conv_out, "height", 2, 1)
     pooled = pool_pairs(moved)
     upsampled = jnp.repeat(cotangent * jnp.asarray(0.5, jnp.bfloat16), 2, axis=0)
     own_rows = n_out // n_rows

time: 318 us -> 309 us (0.972)
  starting transfers between devices: 17.3 us -> 39.7 us
  waiting for transfers between devices: 155 us -> 138 us
  matrix products: 35.4 us -> 20.9 us
    ppermute x0 -> x15, starting transfers between devices: none -> 31 us  [rotated_exchange(): lax.ppermute(sent, axis, [(i, (i + step) % size) for i in range(size)])]
    psum x1, waiting for transfers between devices: 144 us -> 121 us  [local(): summed = lax.psum(jnp.concatenate(blocks, axis=1), ('tm', 'height'))]
    dot_general x9, matrix products: 21.8 us -> 7.32 us  [local(): jnp.einsum('frwk,kc->frcw', patches[tap_t:tap_t + frames, tap_r:tap_r + r...]
    all_to_all x1 -> x0, starting transfers between devices: 8.75 us -> none  [local(): lax.all_to_all(conv_out, 'height', split_axis=2, concat_axis=1, tiled=True)]
    ppermute x0 -> x15, waiting for transfers between devices: none -> 7.09 us  [rotated_exchange(): lax.ppermute(sent, axis, [(i, (i + step) % size) for i in range(size)])]
  transfers between devices with their start and end apart: 5 -> 19, of which waited for: 3 -> 6; matrix products, arithmetic and copies ran while one was open for 3% -> 5% of each run, Pallas kernels for 0% -> 0%
where the time goes in v1:
time: 309 us; the launch traced here: 308 us
  waiting for transfers between devices  138 us (45%)
  blocking collectives  82.2 us (27%)
  starting transfers between devices  39.7 us (13%)
  matrix products  20.9 us (7%)
  between operations  15 us (5%)
  other arithmetic  9.45 us (3%)
    psum x1, waiting for transfers between devices, local(): summed = lax.psum(jnp.concatenate(blocks, axis=1), ('tm', 'height'))  121 us
    psum x1, blocking collectives, local(): group_mean = lax.psum(local_sums, ('tm', 'height')) / entries  42 us
    psum x1, blocking collectives, local(): lax.psum(jnp.sum(centered * centered, axis=(0, 2)), ('tm', 'height'))  40.2 us
    ppermute x15, starting transfers between devices, rotated_exchange(): lax.ppermute(sent, axis, [(i, (i + step) % size) for i in range(size)])  31 us
    dot_general x9, matrix products, local(): jnp.einsum('frwk,frwc->ck', patches[tap_t:tap_t + frames, tap_r:tap_r + r...  13.6 us
    ppermute x1, waiting for transfers between devices, shifted(): lax.ppermute(value, axis, [(source, source + steps) for source in range(f...  10 us
    dot_general x9, matrix products, local(): jnp.einsum('frwk,kc->frcw', patches[tap_t:tap_t + frames, tap_r:tap_r + r...  7.32 us
    ppermute x15, waiting for transfers between devices, rotated_exchange(): lax.ppermute(sent, axis, [(i, (i + step) % size) for i in range(size)])  7.09 us
  transfers between devices with their start and end apart: 19, of which 6 were waited for; matrix products, arithmetic and copies ran while one was open for 5% of the time, Pallas kernels for 0%

profile of v1, /device:TPU:0, one launch (start us, length us, event | category | flops | bytes accessed | tf_op | source)
XLA Modules:
  0.0 308.0 jit_solution(13479069004258072851)
XLA Ops:
  8.8 42.0 %psum.21 = f32[32]{0:T(128)S(1)} all-reduce(f32[32]{0:T(128)S(1)} %reduce_sum.25), channel_id=1, replica_groups=mesh['tm'=2,'height'=16] {'tm','height'}, use_global_device_ids=true, to_apply=%region_2.0 | all-reduce | flops 32 | bytes 256 | tf_op jit(solution)/shard_map/psum | solution.py:73
  52.6 40.2 %psum.22 = f32[32]{0:T(128)S(1)} all-reduce(f32[32]{0:T(128)S(1)} %reduce_sum.37), channel_id=1, replica_groups=mesh['tm'=2,'height'=16] {'tm','height'}, use_global_device_ids=true, to_apply=%region_5.6 | all-reduce | flops 32 | bytes 256 | tf_op jit(solution)/shard_map/psum | solution.py:75
  92.9 1.4 fusion.86
  94.4 4.2 %collective-permute-start = (bf16[2,4,256,128]{3,2,1,0:T(8,128)(2,1)S(1)}, bf16[2,4,256,128]{3,2,1,0:T(8,128)(2,1)S(1)}, u32[]{:S(2)}, u32[]{:S(2)}) collective-permute-start(bf16[2,4,256,128]{3,2,1,0:T(8,128)(2,1)S(1)} %fusion.86), channel_id=1, source_target_pairs={{0,16},{1,17},{2,18},{3,19},{4,20},{5,21},{6,22},{7,23},{8,24},{9,... | collective-permute-start | bytes 1572872 | tf_op jit(solution)/shard_map/ppermute | solution.py:37
  98.8 10.0 %collective-permute-done = bf16[2,4,256,128]{3,2,1,0:T(8,128)(2,1)S(1)} collective-permute-done((bf16[2,4,256,128]{3,2,1,0:T(8,128)(2,1)S(1)}, bf16[2,4,256,128]{3,2,1,0:T(8,128)(2,1)S(1)}, u32[]{:S(2)}, u32[]{:S(2)}) %collective-permute-start) | collective-permute-done | bytes 524320 | tf_op jit(solution)/shard_map/ppermute | solution.py:37
  110.3 3.2 %collective-permute-start.1 = (bf16[4,1,256,128]{3,2,1,0:T(8,128)(2,1)S(1)}, bf16[4,1,256,128]{3,2,1,0:T(8,128)(2,1)S(1)}, u32[]{:S(2)}, u32[]{:S(2)}) collective-permute-start(bf16[4,1,256,128]{3,2,1,0:T(8,128)(2,1)S(1)} %get-tuple-element.19), channel_id=1, source_target_pairs={{0,1},{1,2},{2,3},{3,4},{4,5},{5,6},{6,7},{7,8},{8,9},{9,10},{10,1... | collective-permute-start | bytes 786440 | tf_op jit(solution)/shard_map/ppermute | solution.py:48
  116.0 1.9 pad_maximum_fusion
  125.4 3.3 %collective-permute-start.3 = (bf16[1,2,4,16,256]{4,3,0,2,1:T(8,128)(2,1)S(1)}, bf16[1,2,4,16,256]{4,3,0,2,1:T(8,128)(2,1)S(1)}, u32[]{:S(2)}, u32[]{:S(2)}) collective-permute-start(bf16[1,2,4,16,256]{4,3,0,2,1:T(8,128)(2,1)S(1)} %get-tuple-element.18), channel_id=1, source_target_pairs={{0,1},{1,2},{2,3},{3,4},{4,5},{5,6},{6,7},{7,8},{8,9},{9,10},{10,1... | collective-permute-start | bytes 196616 | tf_op jit(solution)/shard_map/ppermute | solution.py:29
  128.7 2.4 collective-permute-start.4
  131.1 2.1 collective-permute-start.5
  133.2 1.7 collective-permute-start.6
  134.9 1.5 fusion.27
  136.4 1.5 fusion.33
  137.9 1.5 fusion.39
  139.5 1.5 fusion.45
  140.9 1.5 fusion.51
  142.5 1.5 fusion.57
  144.0 1.5 fusion.63
  145.5 1.5 fusion.69
  147.0 1.5 fusion.75
  148.5 1.6 collective-permute-start.8
  150.1 4.1 %collective-permute-start.9 = (bf16[1,2,4,16,256]{4,3,0,2,1:T(8,128)(2,1)S(1)}, bf16[1,2,4,16,256]{4,3,0,2,1:T(8,128)(2,1)S(1)}, u32[]{:S(2)}, u32[]{:S(2)}) collective-permute-start(bf16[1,2,4,16,256]{4,3,0,2,1:T(8,128)(2,1)S(1)} %get-tuple-element.12), channel_id=1, source_target_pairs={{0,7},{1,8},{2,9},{3,10},{4,11},{5,12},{6,13},{7,14},{8,15},{9,0},... | collective-permute-start | bytes 196616 | tf_op jit(solution)/shard_map/ppermute | solution.py:29
  155.1 1.5 collective-permute-start.12
  156.6 2.4 collective-permute-done.8
  159.0 1.8 collective-permute-start.13
  160.8 2.5 collective-permute-start.14
  163.3 2.0 collective-permute-done.10
  165.3 5.5 %collective-permute-start.16 = (bf16[1,2,4,16,256]{4,3,0,2,1:T(8,128)(2,1)S(1)}, bf16[1,2,4,16,256]{4,3,0,2,1:T(8,128)(2,1)S(1)}, u32[]{:S(2)}, u32[]{:S(2)}) collective-permute-start(bf16[1,2,4,16,256]{4,3,0,2,1:T(8,128)(2,1)S(1)} %get-tuple-element.5), channel_id=1, source_target_pairs={{0,14},{1,15},{2,0},{3,1},{4,2},{5,3},{6,4},{7,5},{8,6},{9,7},{10,... | collective-permute-start | bytes 196616 | tf_op jit(solution)/shard_map/ppermute | solution.py:29
  170.8 3.9 %collective-permute-start.17 = (bf16[1,2,4,16,256]{4,3,0,2,1:T(8,128)(2,1)S(1)}, bf16[1,2,4,16,256]{4,3,0,2,1:T(8,128)(2,1)S(1)}, u32[]{:S(2)}, u32[]{:S(2)}) collective-permute-start(bf16[1,2,4,16,256]{4,3,0,2,1:T(8,128)(2,1)S(1)} %get-tuple-element.4), channel_id=1, source_target_pairs={{0,15},{1,0},{2,1},{3,2},{4,3},{5,4},{6,5},{7,6},{8,7},{9,8},{10,9... | collective-permute-start | bytes 196616 | tf_op jit(solution)/shard_map/ppermute | solution.py:29
  174.7 2.7 collective-permute-done.16
  178.5 121.0 %all-reduce.3.cloned.1.call-done = f32[256,3456]{1,0:T(8,128)} async-done(((f32[256,3456]{1,0:T(8,128)}), f32[256,3456]{1,0:T(8,128)}) %all-reduce.3.cloned.1.call-update) | async-done | bytes 3538960 | tf_op jit(solution)/shard_map/psum | solution.py:115
  299.6 1.6 multiply_convert_fusion.1
  (71 shorter events, 16.5 us)
Async XLA Ops:
  7.2 106.6 %copy-start.1 = (bf16[1,4,256,256]{3,2,1,0:T(8,128)(2,1)S(1)}, bf16[1,4,256,256]{3,2,1,0:T(8,128)(2,1)}, u32[]{:S(2)}) copy-start(bf16[1,4,256,256]{3,2,1,0:T(8,128)(2,1)} %param.9) | copy-start | bytes 1572868
  7.2 292.4 %all-reduce.3.cloned.1.call-start = ((), (), s32[]{:S(2)}) async-start(), calls=%async_computation | async-start | bytes 7077888 | tf_op jit(solution)/shard_map/psum | solution.py:115
  94.4 14.5 %collective-permute-start = (bf16[2,4,256,128]{3,2,1,0:T(8,128)(2,1)S(1)}, bf16[2,4,256,128]{3,2,1,0:T(8,128)(2,1)S(1)}, u32[]{:S(2)}, u32[]{:S(2)}) collective-permute-start(bf16[2,4,256,128]{3,2,1,0:T(8,128)(2,1)S(1)} %fusion.86), channel_id=1, source_target_pairs={{0,16},{1,17},{2,18},{3,19},{4,20},{5,21},{6,22},{7,23},{8,24},{9,... | collective-permute-start | bytes 1572872 | tf_op jit(solution)/shard_map/ppermute | solution.py:37
  109.0 5.2 %collective-permute-start.2 = (bf16[4,1,256,128]{3,2,1,0:T(8,128)(2,1)S(1)}, bf16[4,1,256,128]{3,2,1,0:T(8,128)(2,1)S(1)}, u32[]{:S(2)}, u32[]{:S(2)}) collective-permute-start(bf16[4,1,256,128]{3,2,1,0:T(8,128)(2,1)S(1)} %get-tuple-element.20), channel_id=1, source_target_pairs={{1,0},{2,1},{3,2},{4,3},{5,4},{6,5},{7,6},{8,7},{9,8},{10,9},{11,1... | collective-permute-start | bytes 786440 | tf_op jit(solution)/shard_map/ppermute | solution.py:50
  110.3 4.2 %collective-permute-start.1 = (bf16[4,1,256,128]{3,2,1,0:T(8,128)(2,1)S(1)}, bf16[4,1,256,128]{3,2,1,0:T(8,128)(2,1)S(1)}, u32[]{:S(2)}, u32[]{:S(2)}) collective-permute-start(bf16[4,1,256,128]{3,2,1,0:T(8,128)(2,1)S(1)} %get-tuple-element.19), channel_id=1, source_target_pairs={{0,1},{1,2},{2,3},{3,4},{4,5},{5,6},{6,7},{7,8},{8,9},{9,10},{10,1... | collective-permute-start | bytes 786440 | tf_op jit(solution)/shard_map/ppermute | solution.py:48
  116.0 1.9 copy-start
  125.4 23.1 %collective-permute-start.3 = (bf16[1,2,4,16,256]{4,3,0,2,1:T(8,128)(2,1)S(1)}, bf16[1,2,4,16,256]{4,3,0,2,1:T(8,128)(2,1)S(1)}, u32[]{:S(2)}, u32[]{:S(2)}) collective-permute-start(bf16[1,2,4,16,256]{4,3,0,2,1:T(8,128)(2,1)S(1)} %get-tuple-element.18), channel_id=1, source_target_pairs={{0,1},{1,2},{2,3},{3,4},{4,5},{5,6},{6,7},{7,8},{8,9},{9,10},{10,1... | collective-permute-start | bytes 196616 | tf_op jit(solution)/shard_map/ppermute | solution.py:29
  128.7 21.4 %collective-permute-start.4 = (bf16[1,2,4,16,256]{4,3,0,2,1:T(8,128)(2,1)S(1)}, bf16[1,2,4,16,256]{4,3,0,2,1:T(8,128)(2,1)S(1)}, u32[]{:S(2)}, u32[]{:S(2)}) collective-permute-start(bf16[1,2,4,16,256]{4,3,0,2,1:T(8,128)(2,1)S(1)} %get-tuple-element.17), channel_id=1, source_target_pairs={{0,2},{1,3},{2,4},{3,5},{4,6},{5,7},{6,8},{7,9},{8,10},{9,11},{10,... | collective-permute-start | bytes 196616 | tf_op jit(solution)/shard_map/ppermute | solution.py:29
  131.1 23.2 %collective-permute-start.5 = (bf16[1,2,4,16,256]{4,3,0,2,1:T(8,128)(2,1)S(1)}, bf16[1,2,4,16,256]{4,3,0,2,1:T(8,128)(2,1)S(1)}, u32[]{:S(2)}, u32[]{:S(2)}) collective-permute-start(bf16[1,2,4,16,256]{4,3,0,2,1:T(8,128)(2,1)S(1)} %get-tuple-element.16), channel_id=1, source_target_pairs={{0,3},{1,4},{2,5},{3,6},{4,7},{5,8},{6,9},{7,10},{8,11},{9,12},{10... | collective-permute-start | bytes 196616 | tf_op jit(solution)/shard_map/ppermute | solution.py:29
  133.2 21.7 %collective-permute-start.6 = (bf16[1,2,4,16,256]{4,3,0,2,1:T(8,128)(2,1)S(1)}, bf16[1,2,4,16,256]{4,3,0,2,1:T(8,128)(2,1)S(1)}, u32[]{:S(2)}, u32[]{:S(2)}) collective-permute-start(bf16[1,2,4,16,256]{4,3,0,2,1:T(8,128)(2,1)S(1)} %get-tuple-element.15), channel_id=1, source_target_pairs={{0,4},{1,5},{2,6},{3,7},{4,8},{5,9},{6,10},{7,11},{8,12},{9,13},{1... | collective-permute-start | bytes 196616 | tf_op jit(solution)/shard_map/ppermute | solution.py:29
  134.9 20.2 %collective-permute-start.7 = (bf16[1,2,4,16,256]{4,3,0,2,1:T(8,128)(2,1)S(1)}, bf16[1,2,4,16,256]{4,3,0,2,1:T(8,128)(2,1)S(1)}, u32[]{:S(2)}, u32[]{:S(2)}) collective-permute-start(bf16[1,2,4,16,256]{4,3,0,2,1:T(8,128)(2,1)S(1)} %get-tuple-element.14), channel_id=1, source_target_pairs={{0,5},{1,6},{2,7},{3,8},{4,9},{5,10},{6,11},{7,12},{8,13},{9,14},{... | collective-permute-start | bytes 196616 | tf_op jit(solution)/shard_map/ppermute | solution.py:29
  148.5 10.4 %collective-permute-start.8 = (bf16[1,2,4,16,256]{4,3,0,2,1:T(8,128)(2,1)S(1)}, bf16[1,2,4,16,256]{4,3,0,2,1:T(8,128)(2,1)S(1)}, u32[]{:S(2)}, u32[]{:S(2)}) collective-permute-start(bf16[1,2,4,16,256]{4,3,0,2,1:T(8,128)(2,1)S(1)} %get-tuple-element.13), channel_id=1, source_target_pairs={{0,6},{1,7},{2,8},{3,9},{4,10},{5,11},{6,12},{7,13},{8,14},{9,15},... | collective-permute-start | bytes 196616 | tf_op jit(solution)/shard_map/ppermute | solution.py:29
  150.1 10.6 %collective-permute-start.9 = (bf16[1,2,4,16,256]{4,3,0,2,1:T(8,128)(2,1)S(1)}, bf16[1,2,4,16,256]{4,3,0,2,1:T(8,128)(2,1)S(1)}, u32[]{:S(2)}, u32[]{:S(2)}) collective-permute-start(bf16[1,2,4,16,256]{4,3,0,2,1:T(8,128)(2,1)S(1)} %get-tuple-element.12), channel_id=1, source_target_pairs={{0,7},{1,8},{2,9},{3,10},{4,11},{5,12},{6,13},{7,14},{8,15},{9,0},... | collective-permute-start | bytes 196616 | tf_op jit(solution)/shard_map/ppermute | solution.py:29
  154.3 10.9 %collective-permute-start.10 = (bf16[1,2,4,16,256]{4,3,0,2,1:T(8,128)(2,1)S(1)}, bf16[1,2,4,16,256]{4,3,0,2,1:T(8,128)(2,1)S(1)}, u32[]{:S(2)}, u32[]{:S(2)}) collective-permute-start(bf16[1,2,4,16,256]{4,3,0,2,1:T(8,128)(2,1)S(1)} %get-tuple-element.11), channel_id=1, source_target_pairs={{0,8},{1,9},{2,10},{3,11},{4,12},{5,13},{6,14},{7,15},{8,0},{9,1},... | collective-permute-start | bytes 196616 | tf_op jit(solution)/shard_map/ppermute | solution.py:29
  155.0 10.3 %collective-permute-start.11 = (bf16[1,2,4,16,256]{4,3,0,2,1:T(8,128)(2,1)S(1)}, bf16[1,2,4,16,256]{4,3,0,2,1:T(8,128)(2,1)S(1)}, u32[]{:S(2)}, u32[]{:S(2)}) collective-permute-start(bf16[1,2,4,16,256]{4,3,0,2,1:T(8,128)(2,1)S(1)} %get-tuple-element.10), channel_id=1, source_target_pairs={{0,9},{1,10},{2,11},{3,12},{4,13},{5,14},{6,15},{7,0},{8,1},{9,2},... | collective-permute-start | bytes 196616 | tf_op jit(solution)/shard_map/ppermute | solution.py:29
  155.1 15.7 %collective-permute-start.12 = (bf16[1,2,4,16,256]{4,3,0,2,1:T(8,128)(2,1)S(1)}, bf16[1,2,4,16,256]{4,3,0,2,1:T(8,128)(2,1)S(1)}, u32[]{:S(2)}, u32[]{:S(2)}) collective-permute-start(bf16[1,2,4,16,256]{4,3,0,2,1:T(8,128)(2,1)S(1)} %get-tuple-element.9), channel_id=1, source_target_pairs={{0,10},{1,11},{2,12},{3,13},{4,14},{5,15},{6,0},{7,1},{8,2},{9,3},... | collective-permute-start | bytes 196616 | tf_op jit(solution)/shard_map/ppermute | solution.py:29
  159.0 15.7 %collective-permute-start.13 = (bf16[1,2,4,16,256]{4,3,0,2,1:T(8,128)(2,1)S(1)}, bf16[1,2,4,16,256]{4,3,0,2,1:T(8,128)(2,1)S(1)}, u32[]{:S(2)}, u32[]{:S(2)}) collective-permute-start(bf16[1,2,4,16,256]{4,3,0,2,1:T(8,128)(2,1)S(1)} %get-tuple-element.8), channel_id=1, source_target_pairs={{0,11},{1,12},{2,13},{3,14},{4,15},{5,0},{6,1},{7,2},{8,3},{9,4},{... | collective-permute-start | bytes 196616 | tf_op jit(solution)/shard_map/ppermute | solution.py:29
  160.8 13.9 %collective-permute-start.14 = (bf16[1,2,4,16,256]{4,3,0,2,1:T(8,128)(2,1)S(1)}, bf16[1,2,4,16,256]{4,3,0,2,1:T(8,128)(2,1)S(1)}, u32[]{:S(2)}, u32[]{:S(2)}) collective-permute-start(bf16[1,2,4,16,256]{4,3,0,2,1:T(8,128)(2,1)S(1)} %get-tuple-element.7), channel_id=1, source_target_pairs={{0,12},{1,13},{2,14},{3,15},{4,0},{5,1},{6,2},{7,3},{8,4},{9,5},{1... | collective-permute-start | bytes 196616 | tf_op jit(solution)/shard_map/ppermute | solution.py:29
  165.2 9.4 %collective-permute-start.15 = (bf16[1,2,4,16,256]{4,3,0,2,1:T(8,128)(2,1)S(1)}, bf16[1,2,4,16,256]{4,3,0,2,1:T(8,128)(2,1)S(1)}, u32[]{:S(2)}, u32[]{:S(2)}) collective-permute-start(bf16[1,2,4,16,256]{4,3,0,2,1:T(8,128)(2,1)S(1)} %get-tuple-element.6), channel_id=1, source_target_pairs={{0,13},{1,14},{2,15},{3,0},{4,1},{5,2},{6,3},{7,4},{8,5},{9,6},{10... | collective-permute-start | bytes 196616 | tf_op jit(solution)/shard_map/ppermute | solution.py:29
  165.3 12.1 %collective-permute-start.16 = (bf16[1,2,4,16,256]{4,3,0,2,1:T(8,128)(2,1)S(1)}, bf16[1,2,4,16,256]{4,3,0,2,1:T(8,128)(2,1)S(1)}, u32[]{:S(2)}, u32[]{:S(2)}) collective-permute-start(bf16[1,2,4,16,256]{4,3,0,2,1:T(8,128)(2,1)S(1)} %get-tuple-element.5), channel_id=1, source_target_pairs={{0,14},{1,15},{2,0},{3,1},{4,2},{5,3},{6,4},{7,5},{8,6},{9,7},{10,... | collective-permute-start | bytes 196616 | tf_op jit(solution)/shard_map/ppermute | solution.py:29
  170.8 6.6 %collective-permute-start.17 = (bf16[1,2,4,16,256]{4,3,0,2,1:T(8,128)(2,1)S(1)}, bf16[1,2,4,16,256]{4,3,0,2,1:T(8,128)(2,1)S(1)}, u32[]{:S(2)}, u32[]{:S(2)}) collective-permute-start(bf16[1,2,4,16,256]{4,3,0,2,1:T(8,128)(2,1)S(1)} %get-tuple-element.4), channel_id=1, source_target_pairs={{0,15},{1,0},{2,1},{3,2},{4,3},{5,4},{6,5},{7,6},{8,7},{9,8},{10,9... | collective-permute-start | bytes 196616 | tf_op jit(solution)/shard_map/ppermute | solution.py:29
Sparse Core Ops, SparseCore 0:
  148.7 150.8 all-reduce.2
